TPU v7x, 512 devices: a whole 4x4x16 slice. The times are simulated.
512 devices in a mesh: leaf: 32 (over z, core), front: 16 (over y, x).
Axes of the slice: x: 4, y: 4, z: 16, core: 2. Of those that a mesh axis runs over, the one named last changes fastest.
Arguments:
- parent_border_inverse: float32 [32, 1536, 1536], P('leaf', 'front')
- parent_border_rows: float32 [32, 1536, 768], P('leaf', 'front'), may hold values from -0.09 to 0.09
- parent_diagonal_inverse: float32 [32, 768, 768], P('leaf', 'front')
- child_border_rows: float32 [64, 1024, 512], P('leaf', 'front'), may hold values from -0.13 to 0.13
- child_factor_inverse: float32 [64, 512, 512], P('leaf', 'front')
- child_index: int32 [64, 1024], replicated, may hold values from 0 to 2303, as said below
- child_parent: int32 [64], replicated, may hold values from 0 to 31, as said below
Outputs:
- parent_variance: float32 [32, 768], P('leaf')
- child_variance: float32 [64, 512], P('leaf')
Inputs may be any that keep to these rules, and one draw needn't show every extreme that they name: `child_index`: each row holds 1024 distinct positions in increasing order, the first 0 and the last 2303. `child_parent`: child c's parent is c // 2 or c // 2 with its lowest bit flipped, and every parent has exactly two children.
All inputs are finite; a program needn't handle non-finite values.
Results may differ from a plain program's by a relative error of at most 0.0003.
Values sent between devices are 32-bit elements; how exact they have to be, the bound alone decides.
A program may use at most 64 MiB of HBM per device.

v0:
```python
import jax
import jax.numpy as jnp
from jax import lax
from jax.sharding import PartitionSpec as P

ELIMINATED_SIZE = 768
BORDER_SIZE = 1536
CHILD_ELIMINATED = 512


def partner_2(value, axis, distance):
    mask = 2**distance
    pairs = [(source, source ^ mask) for source in range(lax.axis_size(axis))]
    return lax.ppermute(value, axis, pairs)


def matrix_product(left, right):
    return jnp.dot(left, right, precision=lax.Precision.HIGHEST, preferred_element_type=jnp.float32)


def batched_fronts(form, left, right):
    return jnp.einsum(
        form, left, right, precision=lax.Precision.HIGHEST, preferred_element_type=jnp.float32
    )


def folded_rows(left_matrix, block_rows):
    return matrix_product(left_matrix, block_rows)


def children_of(child_parent, owner):
    partner = jnp.bitwise_xor(owner, 1)
    pool_ids = jnp.stack([2 * owner, 2 * owner + 1, 2 * partner, 2 * partner + 1])
    member = (jnp.take(child_parent, pool_ids) == owner).astype(jnp.int32)
    first = jnp.argmax(member)
    second = 3 - jnp.argmax(member[::-1])
    slots = jnp.stack([first, second])
    return (slots, jnp.take(pool_ids, slots))


def shards(
    parent_border_inverse,
    parent_border_rows,
    parent_diagonal_inverse,
    child_border_rows,
    child_factor_inverse,
    child_index,
    child_parent,
):
    border_inverse = parent_border_inverse[0]
    border_factor = parent_border_rows[0]
    eliminated_inverse = parent_diagonal_inverse[0]
    border_rows = border_inverse.shape[0]
    weight_rows = folded_rows(
        border_factor, lax.all_gather(eliminated_inverse, "front", axis=0, tiled=True)
    )
    own_weights = batched_fronts(
        "krj,kjm->krm",
        child_border_rows,
        lax.all_gather(child_factor_inverse, "front", axis=1, tiled=True),
    )
    leaf_index = lax.axis_index("leaf")
    partner = jnp.bitwise_xor(leaf_index, 1)
    partner_weights = partner_2(own_weights, "leaf", 0)
    pooled = jnp.concatenate([own_weights, partner_weights], axis=0)
    slots, kid_ids = children_of(child_parent, leaf_index)
    selected = jnp.take(pooled, slots, axis=0)
    child_weight = lax.all_gather(selected, "front", axis=1, tiled=True)
    index_list = jnp.take(child_index, kid_ids, axis=0)
    placed_rows = (
        jnp.zeros((2, ELIMINATED_SIZE + BORDER_SIZE, CHILD_ELIMINATED), jnp.float32)
        .at[jnp.arange(2)[:, None], index_list]
        .set(child_weight)
    )
    upper_block = placed_rows[:, :ELIMINATED_SIZE]
    lower_block = placed_rows[:, ELIMINATED_SIZE:]
    own_lower = lax.dynamic_slice_in_dim(
        lower_block, lax.axis_index("front") * border_rows, border_rows, 1
    )
    reduced = own_lower - batched_fronts("zt,qtg->qzg", weight_rows, upper_block)
    border_product = folded_rows(
        border_inverse, lax.all_gather(weight_rows, "front", axis=0, tiled=True)
    )
    parent_block = jnp.sum(eliminated_inverse * eliminated_inverse, axis=0) + jnp.sum(
        weight_rows * border_product, axis=0
    )
    kid_image = batched_fronts("rb,kbm->krm", border_inverse, lower_block) - batched_fronts(
        "zt,qtg->qzg", border_product, upper_block
    )
    lifted_rows = batched_fronts("zt,qtg->qzg", eliminated_inverse, upper_block)
    quad_part = jnp.sum(lifted_rows * lifted_rows, axis=1) + jnp.sum(reduced * kid_image, axis=1)
    own_part = jnp.sum(child_factor_inverse * child_factor_inverse, axis=1)
    parent_total, quad_total, own_total = lax.psum((parent_block, quad_part, own_part), "front")
    returned = partner_2(quad_total, "leaf", 0)
    partner_slots, partner_ids = children_of(child_parent, partner)
    mine = 2 * leaf_index + jnp.arange(2, dtype=jnp.int32)
    from_self = (kid_ids[None, :] == mine[:, None]).astype(jnp.float32)
    from_partner = (partner_ids[None, :] == mine[:, None]).astype(jnp.float32)
    kid_quadratic = matrix_product(from_self, quad_total) + matrix_product(from_partner, returned)
    return (parent_total[None], own_total + kid_quadratic)


def solution(mesh):
    in_specs = (
        P("leaf", "front", None),
        P("leaf", "front", None),
        P("leaf", "front", None),
        P("leaf", "front", None),
        P("leaf", "front", None),
        P(),
        P(),
    )
    out_specs = (P("leaf", None), P("leaf", None))
    return jax.shard_map(shards, mesh=mesh, in_specs=in_specs, out_specs=out_specs, check_vma=False)
```

profile of v0, /device:TPU:1, one launch (start us, length us, event | category | flops | bytes accessed | tf_op | source)
XLA Modules:
  0.0 379.8 jit_solution(9751702435656411364)
XLA Ops:
  7.2 0.0 copy-start
  7.2 0.0 copy-start.6
  7.2 0.0 all-gather.8.cloned.1.call-start
  7.2 0.7 all-gather.8.cloned.1.call-update
  7.9 0.0 all-gather.12.cloned.1.call-start
  8.0 0.7 all-gather.12.cloned.1.call-update
  8.7 0.0 all-gather.10.cloned.1.call-start
  8.7 0.1 compare_select_fusion.2
  8.8 0.0 copy-start.7
  8.8 0.0 copy-start.8
  8.8 0.0 copy-start.1
  8.9 1.4 gather_fusion.2
  10.2 0.1 rev.6
  10.3 0.7 iota_reduce_fusion.2
  11.6 0.7 iota_reduce_fusion.3
  12.4 0.0 copy-start.5
  12.4 62.6 %all-gather.8.cloned.1.call-done = f32[2,512,512]{2,1,0:T(8,128)} async-done(((f32[2,32,512]{2,1,0:T(8,128)}), f32[2,512,512]{2,1,0:T(8,128)}) %all-gather.8.cloned.1.call-update) | async-done | bytes 2097168 | tf_op jit(solution)/shard_map/all_gather | solution.py:60
  75.0 3.1 fusion.44
  78.1 4.1 %collective-permute-start = (f32[2,64,512]{2,1,0:T(8,128)S(1)}, f32[2,64,512]{2,1,0:T(8,128)S(1)}, u32[]{:S(2)}, u32[]{:S(2)}) collective-permute-start(f32[2,64,512]{2,1,0:T(8,128)S(1)} %fusion.44), channel_id=1, source_target_pairs={{0,16},{16,0},{32,48},{48,32},{64,80},{80,64},{96,112},{112,96},{1... | collective-permute-start | bytes 786440 | tf_op jit(solution)/shard_map/ppermute | solution.py:14
  82.2 0.8 fusion.38
  83.0 0.8 compare_and_fusion
  83.7 0.0 collective-permute-done
  83.8 0.6 gather_fusion.1
  84.4 0.8 broadcast_select_fusion
  85.2 0.0 all-gather.10.cloned.1.call-update
  85.2 0.0 all-gather.6.cloned.1.call-start
  85.2 53.2 %all-gather.12.cloned.1.call-done = f32[1,768,768]{2,1,0:T(8,128)} async-done(((f32[1,48,768]{2,1,0:T(8,128)}), f32[1,768,768]{2,1,0:T(8,128)}) %all-gather.12.cloned.1.call-update) | async-done | bytes 2359312 | tf_op jit(solution)/shard_map/all_gather | solution.py:55
  138.5 0.0 copy-done.6
  138.5 3.9 %fusion.8 = f32[96,768]{1,0:T(8,128)} fusion(f32[1,768,768]{2,1,0:T(8,128)} %all-gather.12.cloned.1.call-done, f32[1,96,768]{2,1,0:T(8,128)S(1)} %copy-done.6), kind=kOutput, calls=%fused_computation.15 | convolution fusion | flops 679477248 | bytes 2949120 | tf_op jit(solution)/shard_map/dot_general | solution.py:18
  142.3 0.0 all-gather.6.cloned.1.call-update
  142.4 0.6 gather_fusion.3
  143.0 1.5 gather_fusion
  144.6 0.1 compare_select_fusion
  144.6 0.0 copy-done.7
  144.6 0.1 multiply_reduce_fusion.1
  144.7 0.0 copy-done.8
  144.7 0.1 and_reduce_fusion
  144.9 0.0 copy-done.1
  144.9 0.6 gather_fusion.4
  145.5 0.1 rev.7
  145.6 0.7 iota_reduce_fusion
  146.9 0.7 iota_reduce_fusion.1
  147.6 0.7 compare_select_fusion.1
  148.3 0.6 gather_fusion.5
  148.9 0.0 copy-done.5
  149.0 0.0 copy-done.4
  149.0 0.7 and_select_fusion
  149.7 59.2 %all-gather.10.cloned.1.call-done = f32[2,1024,512]{2,1,0:T(8,128)} async-done(((f32[2,64,512]{2,1,0:T(8,128)}), f32[2,1024,512]{2,1,0:T(8,128)}) %all-gather.10.cloned.1.call-update) | async-done | bytes 4194320 | tf_op jit(solution)/shard_map/all_gather | solution.py:68
  208.9 13.8 %scatter_custom_fusion = f32[4608,512]{1,0:T(8,128)} fusion(s32[2048]{0:T(1024)S(1)} %bitcast.76, f32[2048,512]{1,0:T(8,128)} %bitcast.77, f32[]{:T(128)} %constant.46.clone.1), kind=kCustom, calls=%fused_computation.7 | custom fusion | bytes 9437696
  222.7 3.7 slice.21
  226.4 1.8 copy-done.2
  228.2 2.1 fusion.22
  230.3 0.0 copy-done.3
  230.3 2.0 fusion.15
  232.3 48.3 %all-gather.6.cloned.1.call-done = f32[1536,768]{1,0:T(8,128)} async-done(((f32[96,768]{1,0:T(8,128)}), f32[1536,768]{1,0:T(8,128)}) %all-gather.6.cloned.1.call-update) | async-done | bytes 4718608 | tf_op jit(solution)/shard_map/all_gather | solution.py:82
  280.7 0.0 copy-done
  280.7 5.3 %fusion.31 = (f32[768]{0:T(1024)S(1)}, f32[768,96]{0,1:T(8,128)S(1)}) fusion(f32[96,768]{1,0:T(8,128)S(1)} %copy-done.3, f32[1536,768]{1,0:T(8,128)} %all-gather.6.cloned.1.call-done, f32[1,96,1536]{2,1,0:T(8,128)S(1)} %copy-done), kind=kOutput, calls=%fused_computation.34 | convolution fusion | flops 1359101184 | bytes 5901312 | tf_op jit(solution)/shard_map/dot_general | solution.py:18
  286.0 3.9 %fusion.2 = f32[2,512,96]{1,2,0:T(8,128)S(1)} fusion(f32[2,2304,512]{2,1,0:T(8,128)} %bitcast.72, f32[768,96]{0,1:T(8,128)S(1)} %get-tuple-element.24), kind=kOutput, calls=%fused_computation.9 | convolution fusion | flops 905969664 | bytes 3833856 | tf_op jit(solution)/shard_map/zt,qtg->qzg/dot_general | solution.py:22
  289.9 6.7 %fusion.21 = f32[2,512]{1,0:T(2,128)S(1)} fusion(f32[2,96,512]{2,1,0:T(8,128)S(1)} %fusion.15, f32[2,512,96]{1,2,0:T(8,128)S(1)} %fusion.2, f32[1,96,1536]{2,1,0:T(8,128)S(1)} %copy-done, f32[2,2304,512]{2,1,0:T(8,128)} %bitcast.73), kind=kOutput, calls=%fused_computation.23 | convolution fusion | flops 1812233216 | bytes 7671808 | tf_op jit(solution)/shard_map/rb,kbm->krm/dot_general | solution.py:22
  296.6 58.2 %all-reduce = (f32[1,768]{1,0:T(1,128)}, f32[2,512]{1,0:T(2,128)S(1)}, f32[2,512]{1,0:T(2,128)S(1)}) all-reduce(f32[1,768]{1,0:T(1,128)S(1)} %broadcast_in_dim.45, f32[2,512]{1,0:T(2,128)S(1)} %multiply_reduce_fusion, f32[2,512]{1,0:T(2,128)S(1)} %add.91), channel_id=1, replica_groups=mesh['leaf'=32,'front'=16] {'front'}, use_global_device_ids=true, to_apply=%region_2.3 | all-reduce | flops 2816 | bytes 22528 | tf_op jit(solution)/shard_map/psum | solution.py:93
  354.8 16.9 %collective-permute-start.1 = (f32[2,512]{1,0:T(2,128)S(1)}, f32[2,512]{1,0:T(2,128)S(1)}, u32[]{:S(2)}, u32[]{:S(2)}) collective-permute-start(f32[2,512]{1,0:T(2,128)S(1)} %get-tuple-element.14), channel_id=1, source_target_pairs={{0,16},{16,0},{32,48},{48,32},{64,80},{80,64},{96,112},{112,96},{1... | collective-permute-start | bytes 12296 | tf_op jit(solution)/shard_map/ppermute | solution.py:14
  371.7 0.2 fusion.36
  371.9 0.6 collective-permute-done.1
  372.5 0.8 fusion.25
  (23 shorter events, 0.2 us)
Async XLA Ops:
  7.2 273.5 %copy-start = (f32[1,96,1536]{2,1,0:T(8,128)S(1)}, f32[1,96,1536]{2,1,0:T(8,128)}, u32[]{:S(2)}) copy-start(f32[1,96,1536]{2,1,0:T(8,128)} %param.11) | copy-start | bytes 1769476
  7.2 131.3 %copy-start.6 = (f32[1,96,768]{2,1,0:T(8,128)S(1)}, f32[1,96,768]{2,1,0:T(8,128)}, u32[]{:S(2)}) copy-start(f32[1,96,768]{2,1,0:T(8,128)} %param.12) | copy-start | bytes 884740
  7.2 67.8 %all-gather.8.cloned.1.call-start = ((), (), s32[]{:S(2)}) async-start(), calls=%async_computation.1 | async-start | bytes 2228224 | tf_op jit(solution)/shard_map/all_gather | solution.py:60
  7.9 130.5 %all-gather.12.cloned.1.call-start = ((), (), s32[]{:S(2)}) async-start(), calls=%async_computation.3 | async-start | bytes 2506752 | tf_op jit(solution)/shard_map/all_gather | solution.py:55
  8.7 200.2 %all-gather.10.cloned.1.call-start = ((), (), s32[]{:S(2)}) async-start(), calls=%async_computation.2 | async-start | bytes 4456448 | tf_op jit(solution)/shard_map/all_gather | solution.py:68
  8.8 135.8 %copy-start.7 = (s32[2]{0:T(128)S(1)}, s32[2]{0:T(128)}, u32[]{:S(2)}) copy-start(s32[2]{0:T(128)} %constant.94) | copy-start | bytes 28
  8.8 135.9 %copy-start.8 = (s32[2]{0:T(128)S(1)}, s32[2]{0:T(128)}, u32[]{:S(2)}) copy-start(s32[2]{0:T(128)} %constant.97) | copy-start | bytes 28
  8.8 136.0 %copy-start.1 = (s32[64]{0:T(128)S(1)}, s32[64]{0:T(128)}, u32[]{:S(2)}) copy-start(s32[64]{0:T(128)} %param.17) | copy-start | bytes 772
  12.4 136.6 %copy-start.5 = (f32[2,32,512]{2,1,0:T(8,128)S(1)}, f32[2,32,512]{2,1,0:T(8,128)}, u32[]{:S(2)}) copy-start(f32[2,32,512]{2,1,0:T(8,128)} %param.15) | copy-start | bytes 393220
  12.4 136.6 %copy-start.4 = (f32[1,48,768]{2,1,0:T(8,128)S(1)}, f32[1,48,768]{2,1,0:T(8,128)}, u32[]{:S(2)}) copy-start(f32[1,48,768]{2,1,0:T(8,128)} %param.13) | copy-start | bytes 442372
  78.1 5.7 %collective-permute-start = (f32[2,64,512]{2,1,0:T(8,128)S(1)}, f32[2,64,512]{2,1,0:T(8,128)S(1)}, u32[]{:S(2)}, u32[]{:S(2)}) collective-permute-start(f32[2,64,512]{2,1,0:T(8,128)S(1)} %fusion.44), channel_id=1, source_target_pairs={{0,16},{16,0},{32,48},{48,32},{64,80},{80,64},{96,112},{112,96},{1... | collective-permute-start | bytes 786440 | tf_op jit(solution)/shard_map/ppermute | solution.py:14
  85.2 195.5 %all-gather.6.cloned.1.call-start = ((), (), s32[]{:S(2)}) async-start(), calls=%async_computation | async-start | bytes 5013504 | tf_op jit(solution)/shard_map/all_gather | solution.py:82
  222.7 5.5 %copy-start.2 = (f32[4608,512]{1,0:T(8,128)S(1)}, f32[4608,512]{1,0:T(8,128)}, u32[]{:S(2)}) copy-start(f32[4608,512]{1,0:T(8,128)} %scatter_custom_fusion) | copy-start | bytes 28311556
  222.7 7.6 %copy-start.3 = (f32[96,768]{1,0:T(8,128)S(1)}, f32[96,768]{1,0:T(8,128)}, u32[]{:S(2)}) copy-start(f32[96,768]{1,0:T(8,128)} %fusion.8) | copy-start | bytes 884740
  354.8 17.7 %collective-permute-start.1 = (f32[2,512]{1,0:T(2,128)S(1)}, f32[2,512]{1,0:T(2,128)S(1)}, u32[]{:S(2)}, u32[]{:S(2)}) collective-permute-start(f32[2,512]{1,0:T(2,128)S(1)} %get-tuple-element.14), channel_id=1, source_target_pairs={{0,16},{16,0},{32,48},{48,32},{64,80},{80,64},{96,112},{112,96},{1... | collective-permute-start | bytes 12296 | tf_op jit(solution)/shard_map/ppermute | solution.py:14
Sparse Core Ops, SparseCore 0:
  11.0 63.9 all-gather.7
  78.0 60.4 all-gather.11
  141.5 67.3 all-gather.9
  211.7 68.8 all-gather.5
where the time goes:
time: 380 us
  waiting for transfers between devices  225 us (59%)
  blocking collectives  58.2 us (15%)
  matrix products  27.9 us (7%)
  local copies, waits for them, and re-layouts  24.9 us (7%)
  starting transfers between devices  21.2 us (6%)
  between operations  15.3 us (4%)
  other arithmetic  6.92 us (2%)
    all_gather x1, waiting for transfers between devices, shards(): lax.all_gather(child_factor_inverse, 'front', axis=1, tiled=True)  62.6 us
    all_gather x1, waiting for transfers between devices, shards(): child_weight = lax.all_gather(selected, 'front', axis=1, tiled=True)  59.2 us
    psum x1, blocking collectives, shards(): lax.psum((parent_block, quad_part, own_part), 'front')  58.2 us
    all_gather x1, waiting for transfers between devices, shards(): lax.all_gather(eliminated_inverse, 'front', axis=0, tiled=True)  53.2 us
    all_gather x1, waiting for transfers between devices, shards(): lax.all_gather(weight_rows, 'front', axis=0, tiled=True)  48.3 us
    ppermute x2, starting transfers between devices, partner_2(): return lax.ppermute(value, axis, pairs)  21 us
    dot_general x5, matrix products, batched_fronts(): jnp.einsum(form, left, right, precision=lax.Precision.HIGHEST, preferred_...  17.8 us
    unnamed x20, local copies, waits for them, and re-layouts  15.7 us
  transfers between devices with their start and end apart: 6, of which 5 were waited for; matrix products, arithmetic and copies ran while one was open for 11% of the time, Pallas kernels for 0%

commit v1 on v0

--- a/solution.py
+++ b/solution.py
@@ -65,7 +65,9 @@
     pooled = jnp.concatenate([own_weights, partner_weights], axis=0)
     slots, kid_ids = children_of(child_parent, leaf_index)
     selected = jnp.take(pooled, slots, axis=0)
-    child_weight = lax.all_gather(selected, "front", axis=1, tiled=True)
+    child_weight = jnp.concatenate(
+        lax.all_to_all(jnp.stack([selected] * lax.axis_size("front")), "front", 0, 0), axis=1
+    )
     index_list = jnp.take(child_index, kid_ids, axis=0)
     placed_rows = (
         jnp.zeros((2, ELIMINATED_SIZE + BORDER_SIZE, CHILD_ELIMINATED), jnp.float32)

time: 380 us -> 349 us (0.918)
  waiting for transfers between devices: 225 us -> 184 us
  local copies, waits for them, and re-layouts: 24.9 us -> 32.2 us
  starting transfers between devices: 21.2 us -> 26.1 us
    all_to_all x0 -> x1, waiting for transfers between devices: none -> 59.6 us  [shards(): lax.all_to_all(jnp.stack([selected] * lax.axis_size('front')), 'front', 0...]
    all_gather x1 -> x0, waiting for transfers between devices: 59.2 us -> none  [shards(): child_weight = lax.all_gather(selected, 'front', axis=1, tiled=True)]
    all_gather x1, waiting for transfers between devices: 48.3 us -> 0.02 us  [shards(): lax.all_gather(weight_rows, 'front', axis=0, tiled=True)]
    all_gather x1, waiting for transfers between devices: 53.2 us -> 67 us  [shards(): lax.all_gather(eliminated_inverse, 'front', axis=0, tiled=True)]
    all_gather x1, waiting for transfers between devices: 62.6 us -> 55 us  [shards(): lax.all_gather(child_factor_inverse, 'front', axis=1, tiled=True)]
    all_to_all x0 -> x1, starting transfers between devices: none -> 4.86 us  [shards(): lax.all_to_all(jnp.stack([selected] * lax.axis_size('front')), 'front', 0...]
    all_to_all x0 -> x1, local copies, waits for them, and re-layouts: none -> 4.84 us  [shards(): lax.all_to_all(jnp.stack([selected] * lax.axis_size('front')), 'front', 0...]
    unnamed x20 -> x18, local copies, waits for them, and re-layouts: 15.7 us -> 15.7 us
  transfers between devices with their start and end apart: 6 -> 6, of which waited for: 5 -> 4; matrix products, arithmetic and copies ran while one was open for 11% -> 14% of each run, Pallas kernels for 0% -> 0%
where the time goes in v1:
time: 349 us; the launch traced here: 348 us
  waiting for transfers between devices  184 us (53%)
  blocking collectives  56.8 us (16%)
  local copies, waits for them, and re-layouts  32.2 us (9%)
  matrix products  28 us (8%)
  starting transfers between devices  26.1 us (7%)
  between operations  15.3 us (4%)
  other arithmetic  6.04 us (2%)
    all_gather x1, waiting for transfers between devices, shards(): lax.all_gather(eliminated_inverse, 'front', axis=0, tiled=True)  67 us
    all_to_all x1, waiting for transfers between devices, shards(): lax.all_to_all(jnp.stack([selected] * lax.axis_size('front')), 'front', 0...  59.6 us
    psum x1, blocking collectives, shards(): lax.psum((parent_block, quad_part, own_part), 'front')  56.8 us
    all_gather x1, waiting for transfers between devices, shards(): lax.all_gather(child_factor_inverse, 'front', axis=1, tiled=True)  55 us
    ppermute x2, starting transfers between devices, partner_2(): return lax.ppermute(value, axis, pairs)  21.1 us
    dot_general x5, matrix products, batched_fronts(): jnp.einsum(form, left, right, precision=lax.Precision.HIGHEST, preferred_...  17.7 us
    unnamed x18, local copies, waits for them, and re-layouts  15.7 us
    dot_general x4, matrix products, matrix_product(): jnp.dot(left, right, precision=lax.Precision.HIGHEST, preferred_element_t...  10.3 us
  transfers between devices with their start and end apart: 6, of which 4 were waited for; matrix products, arithmetic and copies ran while one was open for 14% of the time, Pallas kernels for 0%

profile of v1, /device:TPU:1, one launch (start us, length us, event | category | flops | bytes accessed | tf_op | source)
XLA Modules:
  0.0 348.2 jit_solution(13975485470752769320)
XLA Ops:
  7.2 0.0 copy-start
  7.2 0.0 all-gather.9.cloned.1.call-start
  7.2 0.7 all-gather.9.cloned.1.call-update
  7.9 0.0 all-gather.7.cloned.1.call-start
  8.0 0.7 all-gather.7.cloned.1.call-update
  8.7 0.0 all-gather.5.cloned.1.call-start
  8.7 67.0 %all-gather.9.cloned.1.call-done = f32[1,768,768]{2,1,0:T(8,128)} async-done(((f32[1,48,768]{2,1,0:T(8,128)}), f32[1,768,768]{2,1,0:T(8,128)}) %all-gather.9.cloned.1.call-update) | async-done | bytes 2359312 | tf_op jit(solution)/shard_map/all_gather | solution.py:55
  75.7 4.0 %fusion.8 = f32[96,768]{1,0:T(8,128)} fusion(f32[1,768,768]{2,1,0:T(8,128)} %all-gather.9.cloned.1.call-done, f32[1,96,768]{2,1,0:T(8,128)} %param.12), kind=kOutput, calls=%fused_computation.15 | convolution fusion | flops 679477248 | bytes 2949120 | tf_op jit(solution)/shard_map/dot_general | solution.py:18
  79.7 0.0 all-gather.5.cloned.1.call-update
  79.7 0.1 compare_select_fusion.2
  79.8 1.3 gather_fusion.2
  81.1 0.1 rev.6
  81.2 0.7 iota_reduce_fusion.2
  82.5 0.7 iota_reduce_fusion.3
  83.2 55.0 %all-gather.7.cloned.1.call-done = f32[2,512,512]{2,1,0:T(8,128)} async-done(((f32[2,32,512]{2,1,0:T(8,128)}), f32[2,512,512]{2,1,0:T(8,128)}) %all-gather.7.cloned.1.call-update) | async-done | bytes 2097168 | tf_op jit(solution)/shard_map/all_gather | solution.py:60
  138.2 3.1 fusion.44
  141.3 4.1 %collective-permute-start = (f32[2,64,512]{2,1,0:T(8,128)S(1)}, f32[2,64,512]{2,1,0:T(8,128)S(1)}, u32[]{:S(2)}, u32[]{:S(2)}) collective-permute-start(f32[2,64,512]{2,1,0:T(8,128)S(1)} %fusion.44), channel_id=1, source_target_pairs={{0,16},{16,0},{32,48},{48,32},{64,80},{80,64},{96,112},{112,96},{1... | collective-permute-start | bytes 786440 | tf_op jit(solution)/shard_map/ppermute | solution.py:14
  145.4 0.7 fusion.38
  146.1 0.7 compare_and_fusion
  146.8 0.0 collective-permute-done
  146.9 0.6 gather_fusion.1
  147.5 0.1 broadcast_select_fusion
  147.6 2.5 stack.80
  150.1 0.0 copy-start.6
  150.1 0.0 copy-start.7
  150.1 0.0 copy-start.1
  150.1 0.0 copy-start.5
  150.1 0.0 copy-start.4
  150.1 4.9 %all-to-all-start = ((f32[16,2,64,512]{3,2,1,0:T(8,128)}), f32[16,2,64,512]{3,2,1,0:T(8,128)}, u32[]{:S(2)}, u32[]{:S(2)}) async-start(f32[16,2,64,512]{3,2,1,0:T(8,128)} %stack.80), calls=%async_computation | async-start | bytes 8388608 | tf_op jit(solution)/shard_map/all_to_all | solution.py:69
  155.0 0.6 gather_fusion.3
  155.6 1.5 gather_fusion
  157.2 0.1 compare_select_fusion
  157.2 0.0 copy-done.6
  157.3 0.1 multiply_reduce_fusion.1
  157.3 0.0 copy-done.7
  157.3 0.1 and_reduce_fusion
  157.5 0.0 copy-done.1
  157.5 0.6 gather_fusion.4
  158.1 0.1 rev.7
  158.2 0.7 iota_reduce_fusion
  159.6 0.7 iota_reduce_fusion.1
  160.2 0.7 compare_select_fusion.1
  160.9 0.6 gather_fusion.5
  161.6 0.0 copy-done.5
  161.6 0.0 copy-done.4
  161.6 0.7 and_select_fusion
  162.3 59.6 %all-to-all-done = f32[16,2,64,512]{3,2,1,0:T(8,128)} async-done(((f32[16,2,64,512]{3,2,1,0:T(8,128)}), f32[16,2,64,512]{3,2,1,0:T(8,128)}, u32[]{:S(2)}, u32[]{:S(2)}) %all-to-all-start) | async-done | bytes 4194336 | tf_op jit(solution)/shard_map/all_to_all | solution.py:69
  222.0 4.8 %copy.9 = f32[16,2,64,512]{3,2,0,1:T(8,128)} copy(f32[16,2,64,512]{3,2,1,0:T(8,128)} %all-to-all-done) | data formatting | bytes 8388608 | tf_op jit(solution)/shard_map/all_to_all | solution.py:69
  226.8 13.8 %scatter_custom_fusion = f32[4608,512]{1,0:T(8,128)} fusion(s32[2048]{0:T(1024)S(1)} %bitcast.79, f32[2048,512]{1,0:T(8,128)} %bitcast.78, f32[]{:T(128)} %constant.46.clone.1), kind=kCustom, calls=%fused_computation.7 | custom fusion | bytes 9437696
  240.6 3.7 %slice.21 = f32[2,1536,512]{2,1,0:T(8,128)S(1)} slice(f32[2,2304,512]{2,1,0:T(8,128)} %bitcast.73), slice={[0:2], [768:2304], [0:512]} | slice | bytes 12582912 | tf_op jit(solution)/shard_map/slice | solution.py:78
  244.3 1.8 copy-done.2
  246.2 2.1 fusion.22
  248.3 0.0 copy-done.3
  248.3 2.0 fusion.15
  250.3 0.0 all-gather.5.cloned.1.call-done
  250.3 0.0 copy-done
  250.3 5.3 %fusion.31 = (f32[768]{0:T(1024)S(1)}, f32[768,96]{0,1:T(8,128)S(1)}) fusion(f32[96,768]{1,0:T(8,128)S(1)} %copy-done.3, f32[1536,768]{1,0:T(8,128)} %all-gather.5.cloned.1.call-done, f32[1,96,1536]{2,1,0:T(8,128)S(1)} %copy-done), kind=kOutput, calls=%fused_computation.34 | convolution fusion | flops 1359101184 | bytes 5901312 | tf_op jit(solution)/shard_map/dot_general | solution.py:18
  255.7 3.9 %fusion.2 = f32[2,512,96]{1,2,0:T(8,128)S(1)} fusion(f32[2,2304,512]{2,1,0:T(8,128)} %bitcast.74, f32[768,96]{0,1:T(8,128)S(1)} %get-tuple-element.24), kind=kOutput, calls=%fused_computation.9 | convolution fusion | flops 905969664 | bytes 3833856 | tf_op jit(solution)/shard_map/zt,qtg->qzg/dot_general | solution.py:22
  259.6 6.7 %fusion.21 = f32[2,512]{1,0:T(2,128)S(1)} fusion(f32[2,96,512]{2,1,0:T(8,128)S(1)} %fusion.15, f32[2,512,96]{1,2,0:T(8,128)S(1)} %fusion.2, f32[1,96,1536]{2,1,0:T(8,128)S(1)} %copy-done, f32[2,2304,512]{2,1,0:T(8,128)} %bitcast.75), kind=kOutput, calls=%fused_computation.23 | convolution fusion | flops 1812233216 | bytes 7671808 | tf_op jit(solution)/shard_map/rb,kbm->krm/dot_general | solution.py:22
  266.3 56.8 %all-reduce = (f32[1,768]{1,0:T(1,128)}, f32[2,512]{1,0:T(2,128)S(1)}, f32[2,512]{1,0:T(2,128)S(1)}) all-reduce(f32[1,768]{1,0:T(1,128)S(1)} %broadcast_in_dim.45, f32[2,512]{1,0:T(2,128)S(1)} %multiply_reduce_fusion, f32[2,512]{1,0:T(2,128)S(1)} %add.91), channel_id=1, replica_groups=mesh['leaf'=32,'front'=16] {'front'}, use_global_device_ids=true, to_apply=%region_2.3 | all-reduce | flops 2816 | bytes 22528 | tf_op jit(solution)/shard_map/psum | solution.py:95
  323.1 17.0 %collective-permute-start.1 = (f32[2,512]{1,0:T(2,128)S(1)}, f32[2,512]{1,0:T(2,128)S(1)}, u32[]{:S(2)}, u32[]{:S(2)}) collective-permute-start(f32[2,512]{1,0:T(2,128)S(1)} %get-tuple-element.14), channel_id=1, source_target_pairs={{0,16},{16,0},{32,48},{48,32},{64,80},{80,64},{96,112},{112,96},{1... | collective-permute-start | bytes 12296 | tf_op jit(solution)/shard_map/ppermute | solution.py:14
  340.1 0.2 fusion.36
  340.3 0.6 collective-permute-done.1
  340.9 0.8 fusion.25
  (22 shorter events, 0.2 us)
Async XLA Ops:
  7.2 243.2 %copy-start = (f32[1,96,1536]{2,1,0:T(8,128)S(1)}, f32[1,96,1536]{2,1,0:T(8,128)}, u32[]{:S(2)}) copy-start(f32[1,96,1536]{2,1,0:T(8,128)} %param.11) | copy-start | bytes 1769476
  7.2 68.5 %all-gather.9.cloned.1.call-start = ((), (), s32[]{:S(2)}) async-start(), calls=%async_computation.3 | async-start | bytes 2506752 | tf_op jit(solution)/shard_map/all_gather | solution.py:55
  7.9 130.3 %all-gather.7.cloned.1.call-start = ((), (), s32[]{:S(2)}) async-start(), calls=%async_computation.2 | async-start | bytes 2228224 | tf_op jit(solution)/shard_map/all_gather | solution.py:60
  8.7 241.7 %all-gather.5.cloned.1.call-start = ((), (), s32[]{:S(2)}) async-start(), calls=%async_computation.1 | async-start | bytes 5013504 | tf_op jit(solution)/shard_map/all_gather | solution.py:84
  141.3 5.5 %collective-permute-start = (f32[2,64,512]{2,1,0:T(8,128)S(1)}, f32[2,64,512]{2,1,0:T(8,128)S(1)}, u32[]{:S(2)}, u32[]{:S(2)}) collective-permute-start(f32[2,64,512]{2,1,0:T(8,128)S(1)} %fusion.44), channel_id=1, source_target_pairs={{0,16},{16,0},{32,48},{48,32},{64,80},{80,64},{96,112},{112,96},{1... | collective-permute-start | bytes 786440 | tf_op jit(solution)/shard_map/ppermute | solution.py:14
  150.1 7.2 %copy-start.6 = (s32[2]{0:T(128)S(1)}, s32[2]{0:T(128)}, u32[]{:S(2)}) copy-start(s32[2]{0:T(128)} %constant.94) | copy-start | bytes 28
  150.1 7.3 %copy-start.7 = (s32[2]{0:T(128)S(1)}, s32[2]{0:T(128)}, u32[]{:S(2)}) copy-start(s32[2]{0:T(128)} %constant.97) | copy-start | bytes 28
  150.1 7.4 %copy-start.1 = (s32[64]{0:T(128)S(1)}, s32[64]{0:T(128)}, u32[]{:S(2)}) copy-start(s32[64]{0:T(128)} %param.17) | copy-start | bytes 772
  150.1 11.5 %copy-start.5 = (f32[2,32,512]{2,1,0:T(8,128)S(1)}, f32[2,32,512]{2,1,0:T(8,128)}, u32[]{:S(2)}) copy-start(f32[2,32,512]{2,1,0:T(8,128)} %param.15) | copy-start | bytes 393220
  150.1 11.5 %copy-start.4 = (f32[1,48,768]{2,1,0:T(8,128)S(1)}, f32[1,48,768]{2,1,0:T(8,128)}, u32[]{:S(2)}) copy-start(f32[1,48,768]{2,1,0:T(8,128)} %param.13) | copy-start | bytes 442372
  150.1 71.9 %all-to-all-start = ((f32[16,2,64,512]{3,2,1,0:T(8,128)}), f32[16,2,64,512]{3,2,1,0:T(8,128)}, u32[]{:S(2)}, u32[]{:S(2)}) async-start(f32[16,2,64,512]{3,2,1,0:T(8,128)} %stack.80), calls=%async_computation | async-start | bytes 8388608 | tf_op jit(solution)/shard_map/all_to_all | solution.py:69
  240.6 5.5 %copy-start.2 = (f32[4608,512]{1,0:T(8,128)S(1)}, f32[4608,512]{1,0:T(8,128)}, u32[]{:S(2)}) copy-start(f32[4608,512]{1,0:T(8,128)} %scatter_custom_fusion) | copy-start | bytes 28311556
  240.6 7.6 %copy-start.3 = (f32[96,768]{1,0:T(8,128)S(1)}, f32[96,768]{1,0:T(8,128)}, u32[]{:S(2)}) copy-start(f32[96,768]{1,0:T(8,128)} %fusion.8) | copy-start | bytes 884740
  323.1 17.8 %collective-permute-start.1 = (f32[2,512]{1,0:T(2,128)S(1)}, f32[2,512]{1,0:T(2,128)S(1)}, u32[]{:S(2)}, u32[]{:S(2)}) collective-permute-start(f32[2,512]{1,0:T(2,128)S(1)} %get-tuple-element.14), channel_id=1, source_target_pairs={{0,16},{16,0},{32,48},{48,32},{64,80},{80,64},{96,112},{112,96},{1... | collective-permute-start | bytes 12296 | tf_op jit(solution)/shard_map/ppermute | solution.py:14
Sparse Core Ops, SparseCore 0:
  11.0 64.6 all-gather.8
  78.7 59.4 all-gather.6
  141.2 105.2 all-gather.4
